TPU v7x, 32 devices: a whole 2x2x4 slice. The times are simulated.
32 devices in a mesh: seq: 8 (over z, core), tp: 4 (over y, x).
Axes of the slice: x: 2, y: 2, z: 4, core: 2. Of those that a mesh axis runs over, the one named last changes fastest.
Arguments:
- qkv: bfloat16 [3, 4, 128, 3072], P(None, None, ('seq', 'tp')), may hold values from -6 to 6
- positions: int32 [3, 4, 128], P(None, None, ('seq', 'tp')), may hold values from 0 to 31, as said below
- w_proj: bfloat16 [3072, 64], replicated, may hold values from -0.21875 to 0.21875
- latents: bfloat16 [4, 128, 64], P(None, 'seq'), may hold values from -6 to 6
- embed_w: bfloat16 [64, 2048], replicated, may hold values from -0.75 to 0.75
- up_w: bfloat16 [2048, 8192], P(None, 'tp'), may hold values from -0.125 to 0.125
- down_w: bfloat16 [8192, 2048], P('tp'), may hold values from -0.0625 to 0.0625
- head_w: bfloat16 [2048, 1000], P(('seq', 'tp')), may hold values from -3 to 3
- labels: int32 [4], replicated, may hold values from 0 to 999
- timesteps: int32 [4], replicated, may hold values from 0 to 999
Outputs:
- guided: bfloat16 [4, 128, 64], P(None, ('seq', 'tp'))
Inputs may be any that keep to these rules, and one draw needn't show every extreme that they name: For each video the tokens are the cells of a stack of frames of 32 x 32 cells, each cell once, in shuffled order; positions[0] is the frame, positions[1] the row, positions[2] the column.
All inputs are finite; a program needn't handle non-finite values.
Results may differ from a plain program's by a relative error of at most 0.0095.
Values may be sent and summed in bfloat16 or wider, within the bound.
No kernel may reach another device: no remote copies, remote signals or barrier semaphores. Data moves between devices by JAX's collectives and lax.ppermute only.
A program may use at most 64 MiB of HBM per device.

v0:
```python
import jax
import jax.numpy as jnp
from jax import lax
from jax.sharding import PartitionSpec as P

HEADS = 24
HEAD_DIM = 128
GUIDANCE = 0.1


def rope_angles(positions, head_dim):
    frame_width = head_dim // 8
    plane_width = (head_dim - frame_width) // 2
    pieces = []
    for axis, width in zip(range(3), (frame_width, plane_width, plane_width)):
        freqs = 10000.0 ** (-jnp.arange(0, width, 2, dtype=jnp.float32) / width)
        pieces.append(positions[axis][..., None] * freqs)
    return jnp.concatenate(pieces, axis=-1)


def rotate(values, angles):
    half = values.shape[-1] // 2
    floats = values.astype(jnp.float32)
    first = floats[..., :half]
    second = floats[..., half:]
    cosine = jnp.cos(angles)[:, :, None, :]
    sine = jnp.sin(angles)[:, :, None, :]
    turned = jnp.concatenate(
        [first * cosine - second * sine, first * sine + second * cosine], axis=-1
    )
    return turned.astype(jnp.bfloat16)


def gelu_slope(values):
    cdf = 0.5 * (1.0 + jax.scipy.special.erf(values * 0.7071067811865476))
    pdf = jnp.exp(-0.5 * values * values) * 0.3989422804014327
    return cdf + values * pdf


def pairs_first(array):
    samples, tokens = (array.shape[0], array.shape[1])
    return array.transpose(0, 2, 1, 3).reshape(samples * HEADS, tokens, HEAD_DIM)


def per_device(qkv, positions, w_proj, latents, embed_w, up_w, down_w, head_w, labels, timesteps):
    samples, tok_dev = (qkv.shape[1], qkv.shape[2])
    angles = rope_angles(positions.astype(jnp.float32), HEAD_DIM)
    shaped = (samples, tok_dev, HEADS, HEAD_DIM)
    queries = rotate(qkv[0].reshape(shaped), angles)
    keys_tok = rotate(qkv[1].reshape(shaped), angles)
    values_tok = qkv[2].reshape(shaped)
    moved = lax.all_to_all(
        jnp.stack([pairs_first(queries), pairs_first(keys_tok), pairs_first(values_tok)]),
        "seq",
        split_axis=1,
        concat_axis=2,
        tiled=True,
    )
    query_pairs = moved[0]
    pair_count, query_count = (query_pairs.shape[0], query_pairs.shape[1])
    running = jnp.full((pair_count, query_count), -jnp.inf, jnp.float32)
    total = jnp.zeros((pair_count, query_count), jnp.float32)
    accum = jnp.zeros((pair_count, query_count, HEAD_DIM), jnp.float32)
    key_piece = lax.all_gather(moved[1], "tp", axis=1, tiled=True)
    value_piece = lax.all_gather(moved[2], "tp", axis=1, tiled=True)
    scores = jnp.einsum(
        "iqd,ikd->iqk", query_pairs, key_piece, preferred_element_type=jnp.float32
    ) * HEAD_DIM ** (-0.5)
    newest = jnp.max(scores, axis=-1)
    factor = jnp.exp(running - newest)
    weights = jnp.exp(scores - newest[..., None])
    total = total * factor + jnp.sum(weights, axis=-1)
    accum = accum * factor[..., None] + jnp.einsum(
        "iqk,ikd->iqd",
        weights.astype(jnp.bfloat16),
        value_piece,
        preferred_element_type=jnp.float32,
    )
    running, total, accum = (newest, total, accum)
    attended = (accum / total[..., None]).astype(jnp.bfloat16)
    returned = lax.all_to_all(attended, "seq", split_axis=1, concat_axis=0, tiled=True)
    returned = returned.reshape(samples, HEADS, tok_dev, HEAD_DIM).transpose(0, 2, 1, 3)
    returned = returned.reshape(samples, tok_dev, HEADS * HEAD_DIM)
    eps = jnp.dot(returned, w_proj, preferred_element_type=jnp.float32)
    seq_len = latents.shape[1] * lax.axis_size("seq")
    tp_index = lax.axis_index("tp")
    emb = jnp.dot(latents, embed_w, preferred_element_type=jnp.float32).astype(jnp.bfloat16)
    hidden = jnp.dot(emb, up_w, preferred_element_type=jnp.float32)
    act = jax.nn.gelu(hidden, approximate=False).astype(jnp.bfloat16)
    branch = jnp.dot(act, down_w, preferred_element_type=jnp.float32)
    own_emb = lax.dynamic_slice_in_dim(emb, tp_index * tok_dev, tok_dev, 1).astype(jnp.float32)
    partial_pool = jnp.sum(branch, axis=1) + jnp.sum(own_emb, axis=1)
    head_rows = head_w.shape[0]
    flat_index = lax.axis_index("seq") * lax.axis_size("tp") + tp_index
    pooled = lax.psum(partial_pool, ("seq", "tp")) / seq_len
    pooled_share = lax.dynamic_slice_in_dim(pooled, flat_index * head_rows, head_rows, 1)
    head_float = head_w.astype(jnp.float32)
    logit_terms = jnp.dot(pooled_share, head_float, precision=lax.Precision.HIGHEST)
    logits = lax.psum(logit_terms, ("seq", "tp"))
    probs = jax.nn.softmax(logits, axis=-1)
    onehot = (labels[:, None] == jnp.arange(logits.shape[1], dtype=jnp.int32)[None, :]).astype(
        jnp.float32
    )
    grad_share = jnp.dot(onehot - probs, head_float.T, precision=lax.Precision.HIGHEST)
    dpool = lax.all_gather(grad_share, ("seq", "tp"), axis=1, tiled=True)
    dact = jnp.dot(dpool, down_w.astype(jnp.float32).T, precision=lax.Precision.HIGHEST)
    dh1 = (gelu_slope(hidden) * dact[:, None, :]).astype(jnp.bfloat16)
    demb = jnp.einsum("btf,cf->btc", dh1, up_w, preferred_element_type=jnp.float32)
    embed_float = embed_w.astype(jnp.float32)
    dx_terms = jnp.einsum("btc,lc->btl", demb, embed_float, precision=lax.Precision.HIGHEST)
    dx_mine = lax.psum_scatter(
        dx_terms.astype(jnp.bfloat16), "tp", scatter_dimension=1, tiled=True
    ).astype(jnp.float32)
    dx_pool = jnp.dot(dpool, embed_float.T, precision=lax.Precision.HIGHEST)
    dx_total = dx_mine + dx_pool[:, None, :]
    phase = (timesteps.astype(jnp.float32) / 1000.0 + 0.008) / 1.008 * (jnp.pi / 2)
    abar = jnp.cos(phase) ** 2
    scale = GUIDANCE * jnp.sqrt(1.0 - abar)
    return (eps - scale[:, None, None] * dx_total).astype(jnp.bfloat16)


def solution(mesh):
    placed = (
        P(None, None, ("seq", "tp"), None),
        P(None, None, ("seq", "tp")),
        P(),
        P(None, "seq", None),
        P(),
        P(None, "tp"),
        P("tp", None),
        P(("seq", "tp"), None),
        P(),
        P(),
    )
    return jax.shard_map(
        per_device,
        mesh=mesh,
        in_specs=placed,
        out_specs=P(None, ("seq", "tp"), None),
        check_vma=False,
    )
```

profile of v0, /device:TPU:0, one launch (start us, length us, event | category | flops | bytes accessed | tf_op | source)
XLA Modules:
  0.0 233.0 jit_solution(14291918177690481106)
XLA Ops:
  0.0 1.1 slice_convert_fusion.1
  1.2 0.1 reshape.93
  1.3 0.1 fusion.126
  1.4 0.7 convert_element_type.55
  2.1 0.1 copy.25
  2.2 0.1 copy.26
  2.3 0.1 copy.24
  2.4 0.1 reshape.94
  2.5 0.1 fusion.127
  2.6 0.1 broadcast_multiply_fusion.2
  2.7 0.1 broadcast_multiply_fusion.1
  2.7 0.2 fusion.124
  2.9 0.1 subtract_convert_fusion.1
  3.0 0.1 pad_maximum_fusion.1
  3.2 0.9 copy.29
  4.1 6.4 %all-to-all-start = ((bf16[3,96,4,128]{3,2,0,1:T(4,128)(2,1)}), bf16[3,96,4,128]{3,2,0,1:T(4,128)(2,1)S(1)}, u32[]{:S(2)}, u32[]{:S(2)}) async-start(bf16[3,96,4,128]{3,2,0,1:T(4,128)(2,1)} %copy.29), calls=%async_computation | async-start | bytes 589824 | tf_op jit(solution)/shard_map/all_to_all | solution.py:52
  10.4 1.2 convolution_convert_fusion
  11.6 5.1 %fusion.72 = (u8[16,2048]{1,0:T(8,128)(4,1)S(1)}, u8[16,2048]{1,0:T(8,128)(4,1)S(1)}, f32[4,16,2048]{2,1,0:T(8,128)S(1)}) fusion(bf16[4,16,2048]{2,1,0:T(8,128)(2,1)S(1)} %convolution_convert_fusion, bf16[2048,2048]{1,0:T(8,128)(2,1)} %param.15), kind=kOutput, calls=%fused_computation.95 | convolution fusion | flops 538509312 | bytes 9240576 | tf_op jit(solution)/shard_map/dot_general | solution.py:88
  16.7 0.1 convert_reduce_fusion
  16.8 0.0 copy-start.2
  16.8 6.0 %fusion.6 = f32[4,2048]{1,0:T(4,128)S(1)} fusion(bf16[2048,2048]{1,0:T(8,128)(2,1)} %param.16, f32[4,16,2048]{2,1,0:T(8,128)S(1)} %get-tuple-element.34, u8[16,2048]{1,0:T(8,128)(4,1)S(1)} %get-tuple-element.6, u8[16,2048]{1,0:T(8,128)(4,1)S(1)} %get-tuple-element.5), kind=kOutput, calls=%fused_computation.7 | convolution fusion | flops 546168832 | bytes 9011200 | tf_op jit(solution)/shard_map/dot_general | solution.py:90
  22.8 40.9 %psum.14 = f32[4,2048]{1,0:T(4,128)S(1)} all-reduce(f32[4,2048]{1,0:T(4,128)S(1)} %add.59), channel_id=1, replica_groups=mesh['seq'=8,'tp'=4] {'seq','tp'}, use_global_device_ids=true, to_apply=%region_4.0 | all-reduce | flops 8192 | bytes 65536 | tf_op jit(solution)/shard_map/psum | solution.py:95
  63.8 0.2 fusion.82
  64.0 40.0 %psum.15 = f32[4,1000]{1,0:T(4,128)S(1)} all-reduce(f32[4,1000]{1,0:T(4,128)S(1)} %fusion.82), channel_id=1, replica_groups=mesh['seq'=8,'tp'=4] {'seq','tp'}, use_global_device_ids=true, to_apply=%region_5.0 | all-reduce | flops 4000 | bytes 32000 | tf_op jit(solution)/shard_map/psum | solution.py:99
  104.0 0.1 reduce_max.19
  104.2 0.2 fusion.78
  104.4 0.2 convolution_bitcast_fusion
  104.6 66.3 %all-gather = f32[32,64,4]{1,2,0:T(4,128)S(1)} all-gather(f32[1,64,4]{1,2,0:T(4,128)S(1)} %convolution_bitcast_fusion), channel_id=1, replica_groups=mesh['seq'=8,'tp'=4] {'seq','tp'}, dimensions={0}, use_global_device_ids=true | all-gather | bytes 33792 | tf_op jit(solution)/shard_map/all_gather | solution.py:105
  170.9 0.1 reshape.88
  171.0 8.9 %fusion.129 = f32[4,2048]{1,0:T(4,128)S(1)} fusion(f32[2048,4]{0,1:T(4,128)S(1)} %reshape.88, bf16[2048,2048]{1,0:T(8,128)(2,1)} %param.16), kind=kOutput, calls=%fused_computation.170 | convolution fusion | flops 201326592 | bytes 8454144 | tf_op jit(solution)/shard_map/dot_general | solution.py:106
  179.9 0.0 copy-start.1
  179.9 6.1 %fusion.2 = f32[4,16,2048]{2,1,0:T(8,128)S(1)} fusion(bf16[2048,2048]{1,0:T(8,128)(2,1)} %param.15, f32[4,16,2048]{2,1,0:T(8,128)S(1)} %get-tuple-element.34, f32[4,2048]{1,0:T(4,128)S(1)} %fusion.129), kind=kOutput, calls=%fused_computation.2 | convolution fusion | flops 538181632 | bytes 9469952 | tf_op jit(solution)/shard_map/btf,cf->btc/dot_general | solution.py:108
  186.0 0.6 dynamic-slice
  187.3 0.4 convolution_convert_fusion.1
  187.7 13.9 %all-reduce = bf16[4,16,64]{2,1,0:T(8,128)(2,1)S(1)} all-reduce(bf16[4,16,64]{2,1,0:T(8,128)(2,1)S(1)} %convolution_convert_fusion.1), channel_id=2, replica_groups=mesh['seq'=8,'tp'=4] {'tp'}, use_global_device_ids=true, to_apply=%region_8.0.clone | all-reduce | flops 4096 | bytes 16384
  201.5 0.3 fusion.130
  201.8 0.1 copy.30
  201.9 0.1 fusion.125
  202.1 8.9 %all_gather.10 = bf16[12,128,128]{2,1,0:T(8,128)(2,1)S(1)} all-gather(bf16[12,32,128]{2,1,0:T(8,128)(2,1)S(1)} %bitcast.77), channel_id=1, replica_groups=mesh['seq'=8,'tp'=4] {'tp'}, dimensions={1}, use_global_device_ids=true | all-gather | bytes 491520 | tf_op jit(solution)/shard_map/all_gather | solution.py:65
  211.1 9.3 %all_gather.9 = bf16[12,128,128]{2,1,0:T(8,128)(2,1)S(1)} all-gather(bf16[12,32,128]{2,1,0:T(8,128)(2,1)S(1)} %bitcast.78), channel_id=1, replica_groups=mesh['seq'=8,'tp'=4] {'tp'}, dimensions={1}, use_global_device_ids=true | all-gather | bytes 491520 | tf_op jit(solution)/shard_map/all_gather | solution.py:64
  220.4 0.4 fusion.128
  220.8 0.2 fusion.69
  221.1 0.3 fusion.10
  221.4 0.7 copy.34
  222.1 3.4 %all-to-all-start.1 = ((bf16[12,32,128]{2,0,1:T(8,128)(2,1)}), bf16[12,32,128]{2,0,1:T(8,128)(2,1)S(1)}, u32[]{:S(2)}, u32[]{:S(2)}) async-start(bf16[12,32,128]{2,0,1:T(8,128)(2,1)} %copy.34), calls=%async_computation.1 | async-start | bytes 262144 | tf_op jit(solution)/shard_map/all_to_all | solution.py:81
  225.5 0.1 sqrt_multiply_fusion
  225.5 6.6 %all-to-all-done.1 = bf16[12,32,128]{2,0,1:T(8,128)(2,1)S(1)} async-done(((bf16[12,32,128]{2,0,1:T(8,128)(2,1)}), bf16[12,32,128]{2,0,1:T(8,128)(2,1)S(1)}, u32[]{:S(2)}, u32[]{:S(2)}) %all-to-all-start.1) | async-done | bytes 98336 | tf_op jit(solution)/shard_map/all_to_all | solution.py:81
  232.2 0.8 fusion.11
  (24 shorter events, 0.3 us)
Async XLA Ops:
  0.0 232.2 %copy-start = (bf16[3072,64]{0,1:T(8,128)(2,1)S(1)}, bf16[3072,64]{0,1:T(8,128)(2,1)}, u32[]{:S(2)}) copy-start(bf16[3072,64]{0,1:T(8,128)(2,1)} %param.12) | copy-start | bytes 1179652
  4.1 197.8 %all-to-all-start = ((bf16[3,96,4,128]{3,2,0,1:T(4,128)(2,1)}), bf16[3,96,4,128]{3,2,0,1:T(4,128)(2,1)S(1)}, u32[]{:S(2)}, u32[]{:S(2)}) async-start(bf16[3,96,4,128]{3,2,0,1:T(4,128)(2,1)} %copy.29), calls=%async_computation | async-start | bytes 589824 | tf_op jit(solution)/shard_map/all_to_all | solution.py:52
  16.8 47.0 %copy-start.2 = (bf16[64,1000]{1,0:T(8,128)(2,1)S(1)}, bf16[64,1000]{1,0:T(8,128)(2,1)}, u32[]{:S(2)}) copy-start(bf16[64,1000]{1,0:T(8,128)(2,1)} %param.17) | copy-start | bytes 384004
  16.8 87.6 %copy-start.3 = (s32[4]{0:T(128)S(1)}, s32[4]{0:T(128)}, u32[]{:S(2)}) copy-start(s32[4]{0:T(128)} %param.18) | copy-start | bytes 52
  179.9 6.1 %copy-start.5 = (u32[32]{0:T(128)S(1)}, u32[32]{0:T(128)}, u32[]{:S(2)}) copy-start(u32[32]{0:T(128)} %constant.123) | copy-start | bytes 388
  179.9 7.4 %copy-start.1 = (bf16[64,2048]{1,0:T(8,128)(2,1)S(1)}, bf16[64,2048]{1,0:T(8,128)(2,1)}, u32[]{:S(2)}) copy-start(bf16[64,2048]{1,0:T(8,128)(2,1)} %param.14) | copy-start | bytes 786436
  179.9 45.5 %copy-start.4 = (s32[4]{0:T(128)S(1)}, s32[4]{0:T(128)}, u32[]{:S(2)}) copy-start(s32[4]{0:T(128)} %param.19) | copy-start | bytes 52
  222.1 10.1 %all-to-all-start.1 = ((bf16[12,32,128]{2,0,1:T(8,128)(2,1)}), bf16[12,32,128]{2,0,1:T(8,128)(2,1)S(1)}, u32[]{:S(2)}, u32[]{:S(2)}) async-start(bf16[12,32,128]{2,0,1:T(8,128)(2,1)} %copy.34), calls=%async_computation.1 | async-start | bytes 262144 | tf_op jit(solution)/shard_map/all_to_all | solution.py:81
where the time goes:
time: 234 us; the launch traced here: 233 us
  blocking collectives  179 us (76%)
  matrix products  29.8 us (13%)
  starting transfers between devices  9.72 us (4%)
  waiting for transfers between devices  6.62 us (3%)
  local copies, waits for them, and re-layouts  3.35 us (1%)
  other arithmetic  3.16 us (1%)
    all_gather x1, blocking collectives, per_device(): dpool = lax.all_gather(grad_share, ('seq', 'tp'), axis=1, tiled=True)  66.3 us
    psum x1, blocking collectives, per_device(): pooled = lax.psum(partial_pool, ('seq', 'tp')) / seq_len  40.9 us
    psum x1, blocking collectives, per_device(): logits = lax.psum(logit_terms, ('seq', 'tp'))  40 us
    unnamed x1, blocking collectives  13.9 us
    all_gather x1, blocking collectives, per_device(): key_piece = lax.all_gather(moved[1], 'tp', axis=1, tiled=True)  9.33 us
    all_gather x1, blocking collectives, per_device(): value_piece = lax.all_gather(moved[2], 'tp', axis=1, tiled=True)  8.92 us
    dot_general x1, matrix products, per_device(): jnp.dot(dpool, down_w.astype(jnp.float32).T, precision=lax.Precision.HIGH...  8.9 us
    all_to_all x1, waiting for transfers between devices, per_device(): lax.all_to_all(attended, 'seq', split_axis=1, concat_axis=0, tiled=True)  6.62 us
  transfers between devices with their start and end apart: 2, of which 1 were waited for; matrix products, arithmetic and copies ran while one was open for 13% of the time, Pallas kernels for 0%

commit v1 on v0

--- a/solution.py
+++ b/solution.py
@@ -1,3 +1,4 @@
+import functools
 import jax
 import jax.numpy as jnp
 from jax import lax
@@ -6,6 +7,23 @@
 HEADS = 24
 HEAD_DIM = 128
 GUIDANCE = 0.1
+
+
+def view_clusters(work_x, axis_id, which_dim):
+    inter, ready = (lax.psum(1, axis_id), lax.axis_index(axis_id))
+    clean, work_now = (work_x, 1)
+    while work_now < inter:
+        before = lax.ppermute(
+            clean, axis_id, tuple(((hop_no, hop_no ^ work_now) for hop_no in range(inter)))
+        )
+        out_arr = jnp.concatenate([clean, before], axis=which_dim)
+        parts_out = jnp.concatenate([before, clean], axis=which_dim)
+        clean = jnp.where(ready & work_now == 0, out_arr, parts_out)
+        work_now = 2 * work_now
+    return clean
+
+
+note_halves = functools.partial(view_clusters, axis_id=("seq", "tp"), which_dim=1)
 
 
 def rope_angles(positions, head_dim):
@@ -102,7 +120,7 @@
         jnp.float32
     )
     grad_share = jnp.dot(onehot - probs, head_float.T, precision=lax.Precision.HIGHEST)
-    dpool = lax.all_gather(grad_share, ("seq", "tp"), axis=1, tiled=True)
+    dpool = note_halves(grad_share)
     dact = jnp.dot(dpool, down_w.astype(jnp.float32).T, precision=lax.Precision.HIGHEST)
     dh1 = (gelu_slope(hidden) * dact[:, None, :]).astype(jnp.bfloat16)
     demb = jnp.einsum("btf,cf->btc", dh1, up_w, preferred_element_type=jnp.float32)

time: 234 us -> 185 us (0.79)
  blocking collectives: 179 us -> 118 us
  waiting for transfers between devices: 6.62 us -> 16 us
  starting transfers between devices: 9.72 us -> 14.8 us
    all_gather x1 -> x0, blocking collectives: 66.3 us -> none  [per_device(): dpool = lax.all_gather(grad_share, ('seq', 'tp'), axis=1, tiled=True)]
    ppermute x0 -> x5, waiting for transfers between devices: none -> 9.64 us  [view_clusters(): lax.ppermute(clean, axis_id, tuple(((hop_no, hop_no ^ work_now) for hop_n...]
    ppermute x0 -> x5, starting transfers between devices: none -> 7.85 us  [view_clusters(): lax.ppermute(clean, axis_id, tuple(((hop_no, hop_no ^ work_now) for hop_n...]
    all_to_all x1, starting transfers between devices: 6.35 us -> 3.56 us  [per_device(): lax.all_to_all(jnp.stack([pairs_first(queries), pairs_first(keys_tok), pa...]
    unnamed x1, blocking collectives: 13.9 us -> 16.6 us
  transfers between devices with their start and end apart: 2 -> 7, of which waited for: 1 -> 5; matrix products, arithmetic and copies ran while one was open for 13% -> 10% of each run, Pallas kernels for 0% -> 0%
where the time goes in v1:
time: 185 us; the launch traced here: 184 us
  blocking collectives  118 us (64%)
  matrix products  29.9 us (16%)
  waiting for transfers between devices  16 us (9%)
  starting transfers between devices  14.8 us (8%)
  local copies, waits for them, and re-layouts  3.25 us (2%)
    psum x1, blocking collectives, per_device(): pooled = lax.psum(partial_pool, ('seq', 'tp')) / seq_len  42.1 us
    psum x1, blocking collectives, per_device(): logits = lax.psum(logit_terms, ('seq', 'tp'))  40.2 us
    unnamed x1, blocking collectives  16.6 us
    all_gather x1, blocking collectives, per_device(): key_piece = lax.all_gather(moved[1], 'tp', axis=1, tiled=True)  10.1 us
    ppermute x5, waiting for transfers between devices, view_clusters(): lax.ppermute(clean, axis_id, tuple(((hop_no, hop_no ^ work_now) for hop_n...  9.64 us
    dot_general x1, matrix products, per_device(): jnp.dot(dpool, down_w.astype(jnp.float32).T, precision=lax.Precision.HIGH...  8.9 us
    all_gather x1, blocking collectives, per_device(): value_piece = lax.all_gather(moved[2], 'tp', axis=1, tiled=True)  8.62 us
    ppermute x5, starting transfers between devices, view_clusters(): lax.ppermute(clean, axis_id, tuple(((hop_no, hop_no ^ work_now) for hop_n...  7.85 us
  transfers between devices with their start and end apart: 7, of which 5 were waited for; matrix products, arithmetic and copies ran while one was open for 10% of the time, Pallas kernels for 0%

profile of v1, /device:TPU:0, one launch (start us, length us, event | category | flops | bytes accessed | tf_op | source)
XLA Modules:
  0.0 184.1 jit_solution(11486707913923413022)
XLA Ops:
  0.0 1.2 convolution_convert_fusion
  1.2 5.1 %fusion.72 = (u8[16,2048]{1,0:T(8,128)(4,1)S(1)}, u8[16,2048]{1,0:T(8,128)(4,1)S(1)}, f32[4,16,2048]{2,1,0:T(8,128)S(1)}) fusion(bf16[4,16,2048]{2,1,0:T(8,128)(2,1)S(1)} %convolution_convert_fusion, bf16[2048,2048]{1,0:T(8,128)(2,1)} %param.15), kind=kOutput, calls=%fused_computation.94 | convolution fusion | flops 538509312 | bytes 9240576 | tf_op jit(solution)/shard_map/dot_general | solution.py:106
  6.3 0.1 convert_reduce_fusion
  6.5 6.0 %fusion.6 = f32[4,2048]{1,0:T(4,128)S(1)} fusion(bf16[2048,2048]{1,0:T(8,128)(2,1)} %param.16, f32[4,16,2048]{2,1,0:T(8,128)S(1)} %get-tuple-element.34, u8[16,2048]{1,0:T(8,128)(4,1)S(1)} %get-tuple-element.6, u8[16,2048]{1,0:T(8,128)(4,1)S(1)} %get-tuple-element.5), kind=kOutput, calls=%fused_computation.7 | convolution fusion | flops 546168832 | bytes 9011200 | tf_op jit(solution)/shard_map/dot_general | solution.py:108
  12.5 42.1 %psum.14 = f32[4,2048]{1,0:T(4,128)S(1)} all-reduce(f32[4,2048]{1,0:T(4,128)S(1)} %add.61), channel_id=1, replica_groups=mesh['seq'=8,'tp'=4] {'seq','tp'}, use_global_device_ids=true, to_apply=%region_4.0 | all-reduce | flops 8192 | bytes 65536 | tf_op jit(solution)/shard_map/psum | solution.py:113
  54.7 0.2 fusion.85
  54.9 40.2 %psum.15 = f32[4,1000]{1,0:T(4,128)S(1)} all-reduce(f32[4,1000]{1,0:T(4,128)S(1)} %fusion.85), channel_id=1, replica_groups=mesh['seq'=8,'tp'=4] {'seq','tp'}, use_global_device_ids=true, to_apply=%region_5.0 | all-reduce | flops 4000 | bytes 32000 | tf_op jit(solution)/shard_map/psum | solution.py:117
  95.1 0.1 reduce_max.19
  95.2 0.2 fusion.79
  95.4 0.2 fusion.77
  95.7 2.3 %collective-permute-start = (f32[4,64]{1,0:T(4,128)S(1)}, f32[4,64]{1,0:T(4,128)S(1)}, u32[]{:S(2)}, u32[]{:S(2)}) collective-permute-start(f32[4,64]{1,0:T(4,128)S(1)} %fusion.77), channel_id=1, source_target_pairs={{0,1},{1,0},{2,3},{3,2},{4,5},{5,4},{6,7},{7,6},{8,9},{9,8},{10,11... | collective-permute-start | bytes 3080 | tf_op jit(solution)/shard_map/ppermute | solution.py:16
  98.1 0.1 reshape.91
  98.2 0.1 fusion.131
  98.3 0.1 copy.24
  98.4 0.1 copy.25
  98.5 0.1 copy.23
  98.6 0.1 reshape.92
  98.7 0.1 fusion.132
  99.0 0.2 fusion.129
  99.1 0.4 collective-permute-done
  99.6 0.1 maximum_select_fusion.6
  99.6 2.0 %collective-permute-start.1 = (f32[4,128]{1,0:T(4,128)S(1)}, f32[4,128]{1,0:T(4,128)S(1)}, u32[]{:S(2)}, u32[]{:S(2)}) collective-permute-start(f32[4,128]{1,0:T(4,128)S(1)} %maximum_select_fusion.6), channel_id=1, source_target_pairs={{0,2},{1,3},{2,0},{3,1},{4,6},{5,7},{6,4},{7,5},{8,10},{9,11},{10,... | collective-permute-start | bytes 6152 | tf_op jit(solution)/shard_map/ppermute | solution.py:16
  101.7 0.1 subtract_convert_fusion.1
  101.8 1.4 collective-permute-done.1
  103.3 0.1 pad_maximum_fusion.1
  103.5 1.0 collective-permute-done.2
  104.4 0.5 collective-permute-start.3
  104.9 0.9 copy.28
  105.8 3.6 %all-to-all-start = ((bf16[3,96,4,128]{3,2,0,1:T(4,128)(2,1)}), bf16[3,96,4,128]{3,2,0,1:T(4,128)(2,1)S(1)}, u32[]{:S(2)}, u32[]{:S(2)}) async-start(bf16[3,96,4,128]{3,2,0,1:T(4,128)(2,1)} %copy.28), calls=%async_computation | async-start | bytes 589824 | tf_op jit(solution)/shard_map/all_to_all | solution.py:70
  109.4 3.0 %collective-permute-start.4 = (f32[4,1024]{1,0:T(4,128)S(1)}, f32[4,1024]{1,0:T(4,128)S(1)}, u32[]{:S(2)}, u32[]{:S(2)}) collective-permute-start(f32[4,1024]{1,0:T(4,128)S(1)} %maximum_select_fusion.1), channel_id=1, source_target_pairs={{0,16},{1,17},{2,18},{3,19},{4,20},{5,21},{6,22},{7,23},{8,24},{9,... | collective-permute-start | bytes 49160 | tf_op jit(solution)/shard_map/ppermute | solution.py:16
  112.4 0.6 dynamic-slice
  113.7 6.8 %collective-permute-done.4 = f32[4,1024]{1,0:T(4,128)S(1)} collective-permute-done((f32[4,1024]{1,0:T(4,128)S(1)}, f32[4,1024]{1,0:T(4,128)S(1)}, u32[]{:S(2)}, u32[]{:S(2)}) %collective-permute-start.4) | collective-permute-done | bytes 16416 | tf_op jit(solution)/shard_map/ppermute | solution.py:16
  120.5 8.9 %fusion.84 = f32[4,2048]{1,0:T(4,128)S(1)} fusion(bf16[2048,2048]{1,0:T(8,128)(2,1)} %param.16, f32[4,1024]{1,0:T(4,128)S(1)} %collective-permute-done.4, f32[4,1024]{1,0:T(4,128)S(1)} %maximum_select_fusion.1, pred[]{:T(512)S(6)} %eq.28), kind=kOutput, calls=%fused_computation.117 | convolution fusion | flops 201351168 | bytes 8454145 | tf_op jit(solution)/shard_map/dot_general | solution.py:124
  129.4 6.1 %fusion.2 = f32[4,16,2048]{2,1,0:T(8,128)S(1)} fusion(bf16[2048,2048]{1,0:T(8,128)(2,1)} %param.15, f32[4,16,2048]{2,1,0:T(8,128)S(1)} %get-tuple-element.34, f32[4,2048]{1,0:T(4,128)S(1)} %fusion.84), kind=kOutput, calls=%fused_computation.2 | convolution fusion | flops 538181632 | bytes 9469952 | tf_op jit(solution)/shard_map/btf,cf->btc/dot_general | solution.py:126
  135.5 0.4 convolution_convert_fusion.1
  135.9 16.6 %all-reduce = bf16[4,16,64]{2,1,0:T(8,128)(2,1)S(1)} all-reduce(bf16[4,16,64]{2,1,0:T(8,128)(2,1)S(1)} %convolution_convert_fusion.1), channel_id=2, replica_groups=mesh['seq'=8,'tp'=4] {'tp'}, use_global_device_ids=true, to_apply=%region_8.9.clone | all-reduce | flops 4096 | bytes 16384
  152.5 0.1 copy.29
  152.6 0.1 fusion.130
  152.7 8.6 %all_gather.7 = bf16[12,128,128]{2,1,0:T(8,128)(2,1)S(1)} all-gather(bf16[12,32,128]{2,1,0:T(8,128)(2,1)S(1)} %bitcast.69), channel_id=1, replica_groups=mesh['seq'=8,'tp'=4] {'tp'}, dimensions={1}, use_global_device_ids=true | all-gather | bytes 491520 | tf_op jit(solution)/shard_map/all_gather | solution.py:83
  161.4 10.1 %all_gather.6 = bf16[12,128,128]{2,1,0:T(8,128)(2,1)S(1)} all-gather(bf16[12,32,128]{2,1,0:T(8,128)(2,1)S(1)} %bitcast.70), channel_id=1, replica_groups=mesh['seq'=8,'tp'=4] {'tp'}, dimensions={1}, use_global_device_ids=true | all-gather | bytes 491520 | tf_op jit(solution)/shard_map/all_gather | solution.py:82
  171.5 0.4 fusion.133
  171.9 0.2 fusion.69
  172.2 0.3 fusion.10
  172.5 0.7 copy.33
  173.2 3.4 %all-to-all-start.1 = ((bf16[12,32,128]{2,0,1:T(8,128)(2,1)}), bf16[12,32,128]{2,0,1:T(8,128)(2,1)S(1)}, u32[]{:S(2)}, u32[]{:S(2)}) async-start(bf16[12,32,128]{2,0,1:T(8,128)(2,1)} %copy.33), calls=%async_computation.1 | async-start | bytes 262144 | tf_op jit(solution)/shard_map/all_to_all | solution.py:99
  176.5 0.3 fusion.83
  176.8 6.4 %all-to-all-done.1 = bf16[12,32,128]{2,0,1:T(8,128)(2,1)S(1)} async-done(((bf16[12,32,128]{2,0,1:T(8,128)(2,1)}), bf16[12,32,128]{2,0,1:T(8,128)(2,1)S(1)}, u32[]{:S(2)}, u32[]{:S(2)}) %all-to-all-start.1) | async-done | bytes 98336 | tf_op jit(solution)/shard_map/all_to_all | solution.py:99
  183.3 0.8 fusion.11
  (39 shorter events, 0.6 us)
Async XLA Ops:
  0.0 183.3 %copy-start = (bf16[3072,64]{0,1:T(8,128)(2,1)S(1)}, bf16[3072,64]{0,1:T(8,128)(2,1)}, u32[]{:S(2)}) copy-start(bf16[3072,64]{0,1:T(8,128)(2,1)} %param.12) | copy-start | bytes 1179652
  6.4 48.3 %copy-start.3 = (bf16[64,1000]{1,0:T(8,128)(2,1)S(1)}, bf16[64,1000]{1,0:T(8,128)(2,1)}, u32[]{:S(2)}) copy-start(bf16[64,1000]{1,0:T(8,128)(2,1)} %param.17) | copy-start | bytes 384004
  6.4 89.0 %copy-start.5 = (s32[4]{0:T(128)S(1)}, s32[4]{0:T(128)}, u32[]{:S(2)}) copy-start(s32[4]{0:T(128)} %param.18) | copy-start | bytes 52
  6.5 91.6 %copy-start.2 = (bf16[3,4,4,3072]{3,2,1,0:T(4,128)(2,1)S(1)}, bf16[3,4,4,3072]{3,2,1,0:T(4,128)(2,1)}, u32[]{:S(2)}) copy-start(bf16[3,4,4,3072]{3,2,1,0:T(4,128)(2,1)} %param.10) | copy-start | bytes 884740
  6.5 91.8 %copy-start.4 = (s32[3,4,4]{2,1,0:T(4,128)S(1)}, s32[3,4,4]{2,1,0:T(4,128)}, u32[]{:S(2)}) copy-start(s32[3,4,4]{2,1,0:T(4,128)} %param.11) | copy-start | bytes 580
  6.5 105.9 %copy-start.6 = (s32[4]{0:T(128)S(1)}, s32[4]{0:T(128)}, u32[]{:S(2)}) copy-start(s32[4]{0:T(128)} %param.19) | copy-start | bytes 52
  6.5 105.9 %copy-start.7 = (u32[32]{0:T(128)S(1)}, u32[32]{0:T(128)}, u32[]{:S(2)}) copy-start(u32[32]{0:T(128)} %constant.129) | copy-start | bytes 388
  95.7 3.9 %collective-permute-start = (f32[4,64]{1,0:T(4,128)S(1)}, f32[4,64]{1,0:T(4,128)S(1)}, u32[]{:S(2)}, u32[]{:S(2)}) collective-permute-start(f32[4,64]{1,0:T(4,128)S(1)} %fusion.77), channel_id=1, source_target_pairs={{0,1},{1,0},{2,3},{3,2},{4,5},{5,4},{6,7},{7,6},{8,9},{9,8},{10,11... | collective-permute-start | bytes 3080 | tf_op jit(solution)/shard_map/ppermute | solution.py:16
  99.6 3.6 %collective-permute-start.1 = (f32[4,128]{1,0:T(4,128)S(1)}, f32[4,128]{1,0:T(4,128)S(1)}, u32[]{:S(2)}, u32[]{:S(2)}) collective-permute-start(f32[4,128]{1,0:T(4,128)S(1)} %maximum_select_fusion.6), channel_id=1, source_target_pairs={{0,2},{1,3},{2,0},{3,1},{4,6},{5,7},{6,4},{7,5},{8,10},{9,11},{10,... | collective-permute-start | bytes 6152 | tf_op jit(solution)/shard_map/ppermute | solution.py:16
  103.3 1.2 collective-permute-start.2
  104.4 4.9 %collective-permute-start.3 = (f32[4,512]{1,0:T(4,128)S(1)}, f32[4,512]{1,0:T(4,128)S(1)}, u32[]{:S(2)}, u32[]{:S(2)}) collective-permute-start(f32[4,512]{1,0:T(4,128)S(1)} %maximum_select_fusion.2), channel_id=1, source_target_pairs={{0,8},{1,9},{2,10},{3,11},{4,12},{5,13},{6,14},{7,15},{8,0},{9,1},... | collective-permute-start | bytes 24584 | tf_op jit(solution)/shard_map/ppermute | solution.py:16
  105.8 46.6 %all-to-all-start = ((bf16[3,96,4,128]{3,2,0,1:T(4,128)(2,1)}), bf16[3,96,4,128]{3,2,0,1:T(4,128)(2,1)S(1)}, u32[]{:S(2)}, u32[]{:S(2)}) async-start(bf16[3,96,4,128]{3,2,0,1:T(4,128)(2,1)} %copy.28), calls=%async_computation | async-start | bytes 589824 | tf_op jit(solution)/shard_map/all_to_all | solution.py:70
  109.4 11.1 %collective-permute-start.4 = (f32[4,1024]{1,0:T(4,128)S(1)}, f32[4,1024]{1,0:T(4,128)S(1)}, u32[]{:S(2)}, u32[]{:S(2)}) collective-permute-start(f32[4,1024]{1,0:T(4,128)S(1)} %maximum_select_fusion.1), channel_id=1, source_target_pairs={{0,16},{1,17},{2,18},{3,19},{4,20},{5,21},{6,22},{7,23},{8,24},{9,... | collective-permute-start | bytes 49160 | tf_op jit(solution)/shard_map/ppermute | solution.py:16
  129.4 6.1 %copy-start.1 = (bf16[64,2048]{1,0:T(8,128)(2,1)S(1)}, bf16[64,2048]{1,0:T(8,128)(2,1)}, u32[]{:S(2)}) copy-start(bf16[64,2048]{1,0:T(8,128)(2,1)} %param.14) | copy-start | bytes 786436
  173.2 10.1 %all-to-all-start.1 = ((bf16[12,32,128]{2,0,1:T(8,128)(2,1)}), bf16[12,32,128]{2,0,1:T(8,128)(2,1)S(1)}, u32[]{:S(2)}, u32[]{:S(2)}) async-start(bf16[12,32,128]{2,0,1:T(8,128)(2,1)} %copy.33), calls=%async_computation.1 | async-start | bytes 262144 | tf_op jit(solution)/shard_map/all_to_all | solution.py:99
